TPU v7x, 128 devices: a whole 4x4x4 slice. The times are simulated.
128 devices in a mesh: grp: 4 (over x), patch: 32 (over z, y, core).
Axes of the slice: x: 4, y: 4, z: 4, core: 2. Of those that a mesh axis runs over, the one named last changes fastest.
Arguments:
- forcing: bfloat16 [4, 1024, 192, 128], P('grp', 'patch'), may hold values from -6 to 6
- stiffness: float32 [4, 1024, 128], P('grp', 'patch'), may hold values from 0.5 to 5
- reaction: float32 [4, 1024, 128], P('grp', 'patch'), may hold values from 0.02 to 0.2
- volumetric: float32 [4, 1024, 128], P('grp', 'patch'), may hold values from 0.2 to 2
- adjacency: int32 [128, 26], replicated, may hold values from 0 to 127
- owner_map: int32 [128, 26], replicated, may hold values from 0 to 31, as said below
- param_scale: float32 [512, 128], replicated, may hold values from 0.25 to 4
- coefficients: float32 [512, 64], replicated, may hold values from -6 to 6
Outputs:
- basis: bfloat16 [4, 1024, 192, 128], P('grp', 'patch')
- block_norms: float32 [32, 512, 256], P('patch', 'grp')
- estimate: float32 [512], P('grp')
Inputs may be any that keep to these rules, and one draw needn't show every extreme that they name: `owner_map`: no subdomain has more than 2 blocks with one owner, and the blocks of one subdomain with one owner stand in consecutive slots; in each group some owner gets exactly 2 blocks from every subdomain of the group.
All inputs are finite; a program needn't handle non-finite values.
Results may differ from a plain program's by a relative error of at most 0.0045.
Values may be sent and summed in bfloat16 or wider, within the bound.
A program may use at most 64 MiB of HBM per device.

v0:
```python
import jax
import jax.numpy as jnp
from jax import lax
from jax.experimental import pallas as pl
from jax.experimental.pallas import tpu as pltpu
from jax.sharding import PartitionSpec as P

MESH = pl.DeviceIdType.MESH
OMEGA = 0.8
EPS = 1e-06
ROWS = 32
K = 64
Z = 128
HALO = 7
VMEM_LIMIT = 62 * 1024 * 1024


def position(i):
    core = i & 1
    y = (i >> 1) & 3
    z = (i >> 3) & 3
    x = i >> 5
    last = jnp.where(core == 0, z, y)
    first = jnp.where(core == 0, y, z)
    return core * 64 + last * 16 + x * 4 + first


def relax_kernel(
    f_hbm, s_hbm, r_hbm, v_hbm,
    basis_hbm, traces_hbm, rows_hbm,
    fext, cells, small, coef, u, spread, out, traces, rows,
    local_sem, halo_send, halo_recv, t_send, t_recv, r_send, r_recv, tp_send, tp_recv, rp_send, rp_recv, out_sem,
):
    x = lax.axis_index("grp")
    p = lax.axis_index("patch")
    c = p % 2
    y = (p // 2) % 4
    z = p // 8
    a = jnp.where(c == 0, z, y)
    b = jnp.where(c == 0, y, z)
    npatch = 32
    right = (p + 1) % npatch
    left = (p + npatch - 1) % npatch
    partner = p + 1 - 2 * c

    def patch_of(last, first):
        return last * (8 - 6 * c) + first * (2 + 6 * c) + c

    firsts = [(x, patch_of(a, (b + d) % 4)) for d in (1, 2, 3)]
    grps = [((x + d) % 4, p) for d in (1, 2, 3)]
    lasts = [(x, patch_of((a + d) % 4, b)) for d in (1, 2, 3)]
    other = (x, partner)

    own_f = pltpu.make_async_copy(f_hbm, fext.at[pl.ds(8, ROWS)], local_sem.at[0])
    own_cells = [
        pltpu.make_async_copy(ref, cells.at[n, pl.ds(8, ROWS)], local_sem.at[1 + n])
        for n, ref in enumerate((s_hbm, r_hbm, v_hbm))
    ]
    own_row = pltpu.make_async_copy(s_hbm.at[pl.ds(ROWS - 1, 1)], rows.at[c, a, x, b], local_sem.at[4])
    for copy in own_cells:
        copy.start()
    own_f.start()
    own_row.start()

    barrier = pltpu.get_barrier_semaphore()
    peers = [(x, left), (x, right)] + firsts + grps + lasts + [other]
    for peer in peers:
        pl.semaphore_signal(barrier, inc=1, device_id=peer, device_id_type=MESH)
    pl.semaphore_wait(barrier, len(peers))

    def remote(src, dst, ssem, rsem, device):
        return pltpu.make_async_remote_copy(
            src_ref=src, dst_ref=dst, send_sem=ssem, recv_sem=rsem, device_id=device, device_id_type=MESH
        )

    to_left, to_right = [], []
    for n, ref in enumerate((s_hbm, r_hbm, v_hbm)):
        to_left.append(
            remote(ref.at[pl.ds(0, 8)], cells.at[n, pl.ds(8 + ROWS, 8)], halo_send.at[0, n], halo_recv.at[0, n], (x, left))
        )
        to_right.append(
            remote(ref.at[pl.ds(ROWS - 8, 8)], cells.at[n, pl.ds(0, 8)], halo_send.at[1, n], halo_recv.at[1, n], (x, right))
        )
    to_left.append(
        remote(f_hbm.at[pl.ds(0, HALO)], fext.at[pl.ds(8 + ROWS, HALO)], halo_send.at[0, 3], halo_recv.at[0, 3], (x, left))
    )
    to_right.append(
        remote(f_hbm.at[pl.ds(ROWS - HALO, HALO)], fext.at[pl.ds(8 - HALO, HALO)], halo_send.at[1, 3], halo_recv.at[1, 3], (x, right))
    )
    for copy in to_left:
        copy.start()
    for copy in to_right:
        copy.start()

    def stage1(buf, ssem, rsem):
        return [remote(buf.at[c, a, x, b], buf.at[c, a, x, b], ssem.at[0, n], rsem.at[0, n], dev) for n, dev in enumerate(firsts)]

    def stage2(buf, ssem, rsem):
        return [remote(buf.at[c, a, x], buf.at[c, a, x], ssem.at[1, n], rsem.at[1, n], dev) for n, dev in enumerate(grps)]

    def stage3(buf, ssem, rsem):
        return [remote(buf.at[c, a], buf.at[c, a], ssem.at[2, n], rsem.at[2, n], dev) for n, dev in enumerate(lasts)]

    def start(copies):
        for copy in copies:
            copy.start()

    own_row.wait()
    r1 = stage1(rows, r_send, r_recv)
    start(r1)

    lane = lax.broadcasted_iota(jnp.int32, (8, Z), 1)
    sub = lax.broadcasted_iota(jnp.int32, (8, Z), 0)

    def coefficients(e0):
        mid = cells[0, pl.ds(e0, 8), :]
        row = sub + e0
        keep_w = jnp.where((row == 8) & (p == 0), 0.0, 1.0)
        keep_e = jnp.where((row == 7 + ROWS) & (p == npatch - 1), 0.0, 1.0)
        keep_s = jnp.where(lane == 0, 0.0, 1.0)
        keep_n = jnp.where(lane == Z - 1, 0.0, 1.0)
        west = 0.5 * (mid + keep_w * cells[0, pl.ds(e0 - 1, 8), :])
        east = 0.5 * (mid + keep_e * cells[0, pl.ds(e0 + 1, 8), :])
        south = 0.5 * (mid + keep_s * pltpu.roll(mid, 1, 1))
        north = 0.5 * (mid + keep_n * pltpu.roll(mid, Z - 1, 1))
        volume = cells[2, pl.ds(e0, 8), :]
        rest = cells[1, pl.ds(e0, 8), :] + west + east + south + north
        diagonal = rest + volume
        weight = OMEGA / diagonal
        values = (
            1.0 - weight * rest,
            1.0 - weight * (rest + 3.0 * volume),
            weight * west * keep_w,
            weight * east * keep_e,
            weight * south * keep_s,
            weight * north * keep_n,
            weight * (1.0 / 3.0),
        )
        for n, value in enumerate(values):
            small[n] = value
        for n in range(7):
            for k in range(8):
                coef[n, e0 + k] = jnp.broadcast_to(small[n, pl.ds(k, 1), :], (8, Z))

    def first_level(e, slot):
        spread[slot] = fext[e].astype(jnp.float32)
        parts = [spread[slot, pl.ds(n, K, stride=3), :].reshape(8, 8, Z) for n in range(3)]
        weight = coef[6, e][None]
        total = parts[0] + parts[1] + parts[2]
        u[0, e, 0:8] = weight * total
        u[0, e, 8:16] = weight * (3.0 * parts[0] - total)
        u[0, e, 16:24] = weight * (3.0 * parts[1] - total)

    def turned(value, shift):
        return pltpu.roll(value.reshape(K, Z), shift, 1).reshape(8, 8, Z)

    def update(level, e, m, before, now, after):
        centre = coef[1 if m == 0 else 0, e][None]
        return (
            u[0, e, pl.ds(8 * m, 8)]
            + centre * now
            + coef[2, e][None] * before
            + coef[3, e][None] * after
            + coef[4, e][None] * turned(now, 1)
            + coef[5, e][None] * turned(now, Z - 1)
        )

    def sweep(level, e0, n):
        for m in range(3):
            part = pl.ds(8 * m, 8)
            before = u[level - 2, e0 - 1, part]
            now = u[level - 2, e0, part]
            for k in range(n):
                after = u[level - 2, e0 + k + 1, part]
                u[level - 1, e0 + k, part] = update(level, e0 + k, m, before, now, after)
                before, now = now, after

    def last_modes(e, count):
        result = []
        for m in range(count):
            part = pl.ds(8 * m, 8)
            result.append(update(8, e, m, u[6, e - 1, part], u[6, e, part], u[6, e + 1, part]))
        return result

    def emit(e, slot):
        total, first, second = last_modes(e, 3)
        values = (total + first, total + second, total - first - second)
        for n, value in enumerate(values):
            spread[slot, pl.ds(n, K, stride=3), :] = value.reshape(K, Z)
        out[e - 8] = spread[slot].astype(jnp.bfloat16)

    for copy in own_cells:
        copy.wait()
    for e0 in (9, 17, 25, 31):
        coefficients(e0)
    own_f.wait()

    def pair_first(i, carry):
        first_level(9 + 2 * i, 0)
        first_level(10 + 2 * i, 1)
        return carry

    lax.fori_loop(0, 15, pair_first, 0)
    for level in range(2, 8):

        def pair(i, carry, level=level):
            sweep(level, 8 + level + 2 * i, 2)
            return carry

        lax.fori_loop(0, 16 - level, pair, 0)

    def finish(copies):
        for copy in copies:
            copy.wait_recv()

    finish(r1)
    r2 = stage2(rows, r_send, r_recv)
    start(r2)

    finish(to_left)
    coefficients(39)

    def right_first(i, carry):
        first_level(39 + 2 * i, 0)
        first_level(40 + 2 * i, 1)
        return carry

    lax.fori_loop(0, 4, right_first, 0)

    def right_level(level, carry):
        sweep(level, 40 - level, 8)
        return carry

    lax.fori_loop(2, 8, right_level, 0)
    total, first = last_modes(7 + ROWS, 2)
    traces[c, a, x, b] = (total + first).reshape(K, Z).astype(jnp.bfloat16)
    finish(r2)
    r3 = stage3(rows, r_send, r_recv)
    start(r3)
    t1 = stage1(traces, t_send, t_recv)
    start(t1)

    finish(to_right)
    coefficients(1)

    def left_first(i, carry):
        first_level(1 + 2 * i, 0)
        first_level(2 + 2 * i, 1)
        return carry

    lax.fori_loop(0, 4, left_first, 0)

    def left_level(level, carry):
        sweep(level, level, 8)
        return carry

    lax.fori_loop(2, 8, left_level, 0)

    finish(t1)
    t2 = stage2(traces, t_send, t_recv)
    start(t2)
    finish(r3)
    rp = remote(rows.at[c], rows.at[c], rp_send, rp_recv, other)
    rp.start()

    def pair_emit(i, carry):
        emit(8 + 2 * i, 0)
        emit(9 + 2 * i, 1)
        return carry

    half = ROWS // 2
    lax.fori_loop(0, half // 2, pair_emit, 0)
    out0 = pltpu.make_async_copy(out.at[pl.ds(0, half)], basis_hbm.at[pl.ds(0, half)], out_sem.at[0])
    out0.start()

    finish(t2)
    t3 = stage3(traces, t_send, t_recv)
    start(t3)

    def slab(k):
        where = (a + 4 - k) % 4
        return remote(traces.at[c, where], traces.at[c, where], tp_send.at[k], tp_recv.at[k], other)

    tp = [slab(k) for k in range(4)]
    tp[0].start()

    lax.fori_loop(half // 2, half, pair_emit, 0)
    out1 = pltpu.make_async_copy(out.at[pl.ds(half, half)], basis_hbm.at[pl.ds(half, half)], out_sem.at[1])
    out1.start()

    for n in (0, 2, 1):
        t3[n].wait_recv()
        tp[n + 1].start()
    finish(tp)
    rp.wait_recv()
    t_out = pltpu.make_async_copy(traces, traces_hbm, out_sem.at[2])
    t_out.start()
    r_out = pltpu.make_async_copy(rows, rows_hbm, out_sem.at[3])
    r_out.start()
    for copy in to_left + to_right + r1 + r2 + r3 + [rp] + t1 + t2 + t3 + tp:
        copy.wait_send()
    for copy in (out0, out1, t_out, r_out):
        copy.wait()


def residual_kernel(table, traces, rows, coeffs_hbm, scales_hbm, norms, partial, coeffs, scales, scales_t, squares, sem):
    g = lax.axis_index("grp")
    quarter = norms.shape[0]
    first = pltpu.make_async_copy(coeffs_hbm.at[pl.ds(g * quarter, quarter)], coeffs, sem.at[0])
    second = pltpu.make_async_copy(scales_hbm.at[pl.ds(g * quarter, quarter)], scales, sem.at[1])
    first.start()
    second.start()
    first.wait()
    second.wait()
    scales_t[...] = scales[...].T
    weights = coeffs[...].astype(jnp.bfloat16)
    contract = (((1,), (1,)), ((), ()))

    def one(i, carry):
        where = position(i)
        scaled = (traces[where].astype(jnp.float32) * rows[where]).astype(jnp.bfloat16)
        own = scales_t[pl.ds(i, 1), :]
        for k in range(2):
            entry = table[2 * i + k]
            j = jnp.maximum(entry, 0)
            live = jnp.where(entry >= 0, 1.0, 0.0).astype(jnp.float32)
            other = traces[position(j)]
            block = lax.dot_general(scaled, other, contract, preferred_element_type=jnp.float32)
            turned = lax.dot_general(other, scaled, contract, preferred_element_type=jnp.float32)
            forward = lax.dot_general(block.astype(jnp.bfloat16), weights, contract, preferred_element_type=jnp.float32)
            backward = lax.dot_general(turned.astype(jnp.bfloat16), weights, contract, preferred_element_type=jnp.float32)
            residual = own * forward - scales_t[pl.ds(j, 1), :] * backward
            squares[pl.ds(2 * i + k, 1), :] = jnp.sum(residual * residual, axis=0, keepdims=True) * live
        return carry

    lax.fori_loop(0, traces.shape[0], one, 0)
    every = squares[...]
    partial[...] = jnp.sum(every, axis=0, keepdims=True)
    norms[...] = jnp.sqrt(every.T + EPS)


def total_kernel(mine, total, inbox, send_sem, recv_sem, own_sem):
    x = lax.axis_index("grp")
    p = lax.axis_index("patch")
    count = inbox.shape[0]
    own = pltpu.make_async_copy(mine, inbox.at[p], own_sem)
    own.start()
    barrier = pltpu.get_barrier_semaphore()
    for d in range(1, count):
        pl.semaphore_signal(barrier, inc=1, device_id=(x, (p + d) % count), device_id_type=MESH)
    pl.semaphore_wait(barrier, count - 1)
    copies = []
    for d in range(1, count):
        copies.append(
            pltpu.make_async_remote_copy(
                src_ref=mine, dst_ref=inbox.at[p], send_sem=send_sem.at[d - 1], recv_sem=recv_sem.at[d - 1],
                device_id=(x, (p + d) % count), device_id_type=MESH,
            )
        )
    for copy in copies:
        copy.start()
    own.wait()
    for copy in copies:
        copy.wait_recv()
    value = inbox[0]
    for d in range(1, count):
        value = value + inbox[d]
    total[...] = value
    for copy in copies:
        copy.wait_send()


def owned(owner_map, adjacency, owner):
    mine = owner_map == owner
    earlier = jnp.pad(mine, ((0, 0), (1, 0)))[:, :-1]
    picked = jnp.stack([mine & ~earlier, mine & earlier], axis=1)
    found = jnp.sum(jnp.where(picked, adjacency[:, None, :] + 1, 0), axis=2)
    return (found - 1).reshape(-1)


def body(forcing, stiffness, reaction, volumetric, adjacency, owner_map, param_scale, coefficients):
    anywhere = pl.BlockSpec(memory_space=pl.ANY)
    vmem = pl.BlockSpec(memory_space=pltpu.VMEM)
    dma = pltpu.SemaphoreType.DMA
    f32, bf16 = jnp.float32, jnp.bfloat16
    params = pltpu.CompilerParams(collective_id=0, has_side_effects=True, vmem_limit_bytes=VMEM_LIMIT)
    basis, traces, rows = pl.pallas_call(
        relax_kernel,
        name="relax",
        out_shape=(
            jax.ShapeDtypeStruct((ROWS, 3 * K, Z), bf16),
            jax.ShapeDtypeStruct((2, 4, 4, 4, K, Z), bf16),
            jax.ShapeDtypeStruct((2, 4, 4, 4, 1, Z), f32),
        ),
        in_specs=[anywhere] * 4,
        out_specs=(anywhere,) * 3,
        scratch_shapes=[
            pltpu.VMEM((48, 3 * K, Z), bf16),
            pltpu.VMEM((3, 48, Z), f32),
            pltpu.VMEM((7, 8, Z), f32),
            pltpu.VMEM((7, 48, 8, Z), f32),
            pltpu.VMEM((7, 48, 24, 8, Z), f32),
            pltpu.VMEM((2, 3 * K, Z), f32),
            pltpu.VMEM((ROWS, 3 * K, Z), bf16),
            pltpu.VMEM((2, 4, 4, 4, K, Z), bf16),
            pltpu.VMEM((2, 4, 4, 4, 1, Z), f32),
            dma((5,)),
            dma((2, 4)),
            dma((2, 4)),
            dma((3, 3)),
            dma((3, 3)),
            dma((3, 3)),
            dma((3, 3)),
            dma((4,)),
            dma((4,)),
            dma,
            dma,
            dma((4,)),
        ],
        compiler_params=params,
    )(forcing[0], stiffness[0], reaction[0], volumetric[0])

    patch = lax.axis_index("patch")
    table = owned(owner_map, adjacency, patch)
    quarter = param_scale.shape[0] // 4
    slots = table.shape[0]
    norms, partial = pl.pallas_call(
        residual_kernel,
        name="residual",
        out_shape=(jax.ShapeDtypeStruct((quarter, slots), f32), jax.ShapeDtypeStruct((1, quarter), f32)),
        in_specs=[pl.BlockSpec(memory_space=pltpu.SMEM), vmem, vmem, anywhere, anywhere],
        out_specs=(vmem, vmem),
        scratch_shapes=[
            pltpu.VMEM((quarter, K), f32),
            pltpu.VMEM((quarter, param_scale.shape[1]), f32),
            pltpu.VMEM((param_scale.shape[1], quarter), f32),
            pltpu.VMEM((slots, quarter), f32),
            dma((2,)),
        ],
    )(table, traces.reshape(-1, K, Z), rows.reshape(-1, 1, Z), coefficients, param_scale)

    npatch = lax.axis_size("patch")
    total = pl.pallas_call(
        total_kernel,
        name="total",
        out_shape=jax.ShapeDtypeStruct((1, quarter), f32),
        in_specs=[vmem],
        out_specs=vmem,
        scratch_shapes=[pltpu.VMEM((npatch, 1, quarter), f32), dma((npatch - 1,)), dma((npatch - 1,)), dma],
        compiler_params=pltpu.CompilerParams(collective_id=1, has_side_effects=True),
    )(partial)
    estimate = jnp.sqrt(total[0] + EPS)
    return (basis[None], norms[None], estimate)


def solution(mesh):
    placed = (
        P("grp", "patch", None, None),
        P("grp", "patch", None),
        P("grp", "patch", None),
        P("grp", "patch", None),
        P(),
        P(),
        P(),
        P(),
    )
    return jax.shard_map(
        body,
        mesh=mesh,
        in_specs=placed,
        out_specs=(P("grp", "patch", None, None), P("patch", "grp", None), P("grp")),
        check_vma=False,
    )
```

profile of v0, /device:TPU:1, one launch (start us, length us, event | category | flops | bytes accessed | tf_op | source)
XLA Modules:
  0.0 123.4 jit_solution(10957953452717597893)
XLA Ops:
  0.6 0.0 copy-start.2
  0.6 0.0 copy-start.3
  0.7 0.0 copy-start.1
  0.7 53.0 %relax.1 = (bf16[32,192,128]{2,1,0:T(8,128)(2,1)}, bf16[2,4,4,4,64,128]{5,4,3,2,1,0:T(8,128)(2,1)}, f32[2,4,4,4,1,128]{5,4,3,2,1,0:T(1,128)}) custom-call(bf16[32,192,128]{2,1,0:T(8,128)(2,1)} %bitcast.15, f32[32,128]{1,0:T(8,128)} %bitcast.18, f32[32,128]{1,0:T(8,128)} %bitcast.19, f32[32,128]{1,0:T(8,128)} %bitcast.20), custom_call_target="tpu_custom_call" | custom-call | tf_op jit(solution)/shard_map/relax/pallas_call | solution.py:387
  53.6 0.0 copy-done.2
  53.7 0.0 copy-done.3
  53.7 0.1 copy.13
  53.8 0.0 copy-start
  53.9 0.7 sub.7.table
  54.5 0.0 copy-done.1
  54.5 0.8 copy.14.coeffs_hbm
  55.4 56.8 %residual.1 = (f32[128,256]{1,0:T(8,128)}, f32[1,128]{1,0:T(1,128)}) custom-call(s32[256]{0:T(256)} %sub.7.table, bf16[128,64,128]{2,1,0:T(8,128)(2,1)} %bitcast.14, f32[128,1,128]{2,1,0:T(1,128)} %bitcast.17, f32[512,64]{1,0:T(8,128)} %copy.14.coeffs_hbm, f32[512,128]{1,0:T(8,128)} %scales_hbm.1), custom_call_target="tpu_custom_call" | custom-call | tf_op jit(solution)/shard_map/residual/pallas_call | solution.py:427
  112.2 8.9 %total.1 = f32[1,128]{1,0:T(1,128)} custom-call(f32[1,128]{1,0:T(1,128)} %get-tuple-element.12.mine), custom_call_target="tpu_custom_call" | custom-call | tf_op jit(solution)/shard_map/total/pallas_call | solution.py:443
  121.1 1.1 sqrt_bitcast_fusion
  122.2 0.0 copy-done
  122.2 1.1 copy.16
  (5 shorter events, 0.1 us)
Async XLA Ops:
  0.6 53.0 %copy-start.2 = (s32[128,26]{0,1:T(8,128)S(1)}, s32[128,26]{0,1:T(8,128)}, u32[]{:S(2)}) copy-start(s32[128,26]{0,1:T(8,128)} %param.13) | copy-start | bytes 39940
  0.6 53.0 %copy-start.3 = (s32[128,26]{0,1:T(8,128)S(1)}, s32[128,26]{0,1:T(8,128)}, u32[]{:S(2)}) copy-start(s32[128,26]{0,1:T(8,128)} %param.12) | copy-start | bytes 39940
  0.7 53.9 %copy-start.1 = (f32[512,64]{0,1:T(8,128)S(1)}, f32[512,64]{0,1:T(8,128)}, u32[]{:S(2)}) copy-start(f32[512,64]{0,1:T(8,128)} %param.15) | copy-start | bytes 393220
  53.8 68.4 %copy-start = (bf16[32,192,128]{2,1,0:T(8,128)(2,1)S(1)}, bf16[32,192,128]{2,1,0:T(8,128)(2,1)}, u32[]{:S(2)}) copy-start(bf16[32,192,128]{2,1,0:T(8,128)(2,1)} %get-tuple-element.8) | copy-start | bytes 4718596
where the time goes:
time: 124 us; the launch traced here: 123 us
  Pallas kernels  119 us (96%)
  local copies, waits for them, and re-layouts  2.79 us (2%)
    pallas_call x1, Pallas kernels, body(): pl.pallas_call(residual_kernel, name='residual', out_shape=(jax.ShapeDtyp...  56.8 us
    pallas_call x1, Pallas kernels, body(): pl.pallas_call(relax_kernel, name='relax', out_shape=(jax.ShapeDtypeStruc...  53 us
    pallas_call x1, Pallas kernels, body(): pl.pallas_call(total_kernel, name='total', out_shape=jax.ShapeDtypeStruct...  8.9 us

commit v1 on v0

v1 whole, which is shorter than its diff:
```python
import jax
import jax.numpy as jnp
from jax import lax
from jax.experimental import pallas as pl
from jax.experimental.pallas import tpu as pltpu
from jax.sharding import PartitionSpec as P

MESH = pl.DeviceIdType.MESH
OMEGA = 0.8
EPS = 1e-06
ROWS = 32
K = 64
Z = 128
HALO = 7
VMEM_LIMIT = 62 * 1024 * 1024


def position(i):
    core = i & 1
    y = (i >> 1) & 3
    z = (i >> 3) & 3
    x = i >> 5
    last = jnp.where(core == 0, z, y)
    first = jnp.where(core == 0, y, z)
    return core * 64 + last * 16 + x * 4 + first


def round_kernel(
    table, f_hbm, s_hbm, r_hbm, v_hbm, coeffs_hbm, scales_hbm,
    basis_hbm, norms, estimate,
    u0, u1, u2, u3, u4, u5, u6,
    fext, cells, small, coef, spread, out, traces, rows,
    coeffs, scales, scales_t, wide, weights, weights2, fw0, bw0, fw1, bw1, parts, inbox,
    local_sem, halo_send, halo_recv, t_send, t_recv, r_send, r_recv, tp_send, tp_recv, rp_send, rp_recv, out_sem,
    s_send, s_recv,
):
    x = lax.axis_index("grp")
    p = lax.axis_index("patch")
    c = p % 2
    y = (p // 2) % 4
    z = p // 8
    a = jnp.where(c == 0, z, y)
    b = jnp.where(c == 0, y, z)
    npatch = 32
    u = (u0, u1, u2, u3, u4, u5, u6)
    line = c * 64 + a * 16
    plane = line + x * 4
    place = plane + b
    right = (p + 1) % npatch
    left = (p + npatch - 1) % npatch
    partner = p + 1 - 2 * c

    def patch_of(last, first):
        return last * (8 - 6 * c) + first * (2 + 6 * c) + c

    firsts = [(x, patch_of(a, (b + d) % 4)) for d in (1, 2, 3)]
    grps = [((x + d) % 4, p) for d in (1, 2, 3)]
    lasts = [(x, patch_of((a + d) % 4, b)) for d in (1, 2, 3)]
    other = (x, partner)

    own_f = pltpu.make_async_copy(f_hbm, fext.at[pl.ds(8, ROWS)], local_sem.at[0])
    own_cells = [
        pltpu.make_async_copy(ref, cells.at[n, pl.ds(8, ROWS)], local_sem.at[1 + n])
        for n, ref in enumerate((s_hbm, r_hbm, v_hbm))
    ]
    own_row = pltpu.make_async_copy(s_hbm.at[pl.ds(ROWS - 1, 1)], rows.at[place], local_sem.at[4])
    quarter = norms.shape[0]
    own_p = [
        pltpu.make_async_copy(coeffs_hbm.at[pl.ds(x * quarter, quarter)], coeffs, local_sem.at[5]),
        pltpu.make_async_copy(scales_hbm.at[pl.ds(x * quarter, quarter)], scales, local_sem.at[6]),
    ]
    for copy in own_cells + [own_f, own_row] + own_p:
        copy.start()

    barrier = pltpu.get_barrier_semaphore()
    peers = [(x, left), (x, right)] + firsts + grps + lasts + [other]
    for peer in peers:
        pl.semaphore_signal(barrier, inc=1, device_id=peer, device_id_type=MESH)
    pl.semaphore_wait(barrier, len(peers))

    def remote(src, dst, ssem, rsem, device):
        return pltpu.make_async_remote_copy(
            src_ref=src, dst_ref=dst, send_sem=ssem, recv_sem=rsem, device_id=device, device_id_type=MESH
        )

    to_left, to_right = [], []
    for n, ref in enumerate((s_hbm, r_hbm, v_hbm)):
        to_left.append(
            remote(ref.at[pl.ds(0, 8)], cells.at[n, pl.ds(8 + ROWS, 8)], halo_send.at[0, n], halo_recv.at[0, n], (x, left))
        )
        to_right.append(
            remote(ref.at[pl.ds(ROWS - 8, 8)], cells.at[n, pl.ds(0, 8)], halo_send.at[1, n], halo_recv.at[1, n], (x, right))
        )
    to_left.append(
        remote(f_hbm.at[pl.ds(0, HALO)], fext.at[pl.ds(8 + ROWS, HALO)], halo_send.at[0, 3], halo_recv.at[0, 3], (x, left))
    )
    to_right.append(
        remote(f_hbm.at[pl.ds(ROWS - HALO, HALO)], fext.at[pl.ds(8 - HALO, HALO)], halo_send.at[1, 3], halo_recv.at[1, 3], (x, right))
    )
    for copy in to_left:
        copy.start()
    for copy in to_right:
        copy.start()

    def stage1(buf, ssem, rsem):
        return [remote(buf.at[place], buf.at[place], ssem.at[0, n], rsem.at[0, n], dev) for n, dev in enumerate(firsts)]

    def stage2(buf, ssem, rsem):
        return [remote(buf.at[pl.ds(plane, 4)], buf.at[pl.ds(plane, 4)], ssem.at[1, n], rsem.at[1, n], dev) for n, dev in enumerate(grps)]

    def stage3(buf, ssem, rsem):
        return [remote(buf.at[pl.ds(line, 16)], buf.at[pl.ds(line, 16)], ssem.at[2, n], rsem.at[2, n], dev) for n, dev in enumerate(lasts)]

    def start(copies):
        for copy in copies:
            copy.start()

    own_row.wait()
    r1 = stage1(rows, r_send, r_recv)
    start(r1)

    lane = lax.broadcasted_iota(jnp.int32, (8, Z), 1)
    sub = lax.broadcasted_iota(jnp.int32, (8, Z), 0)

    def coefficients(e0):
        mid = cells[0, pl.ds(e0, 8), :]
        row = sub + e0
        keep_w = jnp.where((row == 8) & (p == 0), 0.0, 1.0)
        keep_e = jnp.where((row == 7 + ROWS) & (p == npatch - 1), 0.0, 1.0)
        keep_s = jnp.where(lane == 0, 0.0, 1.0)
        keep_n = jnp.where(lane == Z - 1, 0.0, 1.0)
        west = 0.5 * (mid + keep_w * cells[0, pl.ds(e0 - 1, 8), :])
        east = 0.5 * (mid + keep_e * cells[0, pl.ds(e0 + 1, 8), :])
        south = 0.5 * (mid + keep_s * pltpu.roll(mid, 1, 1))
        north = 0.5 * (mid + keep_n * pltpu.roll(mid, Z - 1, 1))
        volume = cells[2, pl.ds(e0, 8), :]
        rest = cells[1, pl.ds(e0, 8), :] + west + east + south + north
        diagonal = rest + volume
        weight = OMEGA / diagonal
        values = (
            1.0 - weight * rest,
            1.0 - weight * (rest + 3.0 * volume),
            weight * west * keep_w,
            weight * east * keep_e,
            weight * south * keep_s,
            weight * north * keep_n,
            weight * (1.0 / 3.0),
        )
        for n, value in enumerate(values):
            small[n] = value
        for n in range(7):
            for k in range(8):
                coef[n, e0 + k] = jnp.broadcast_to(small[n, pl.ds(k, 1), :], (8, Z))

    def first_level(e, slot):
        spread[slot] = fext[e].astype(jnp.float32)
        parts = [spread[slot, pl.ds(n, K, stride=3), :].reshape(8, 8, Z) for n in range(3)]
        weight = coef[6, e][None]
        total = parts[0] + parts[1] + parts[2]
        u0[e, 0:8] = weight * total
        u0[e, 8:16] = weight * (3.0 * parts[0] - total)
        u0[e, 16:24] = weight * (3.0 * parts[1] - total)

    def turned(value, shift):
        return pltpu.roll(value.reshape(K, Z), shift, 1).reshape(8, 8, Z)

    def update(level, e, m, before, now, after):
        centre = coef[1 if m == 0 else 0, e][None]
        return (
            u0[e, pl.ds(8 * m, 8)]
            + centre * now
            + coef[2, e][None] * before
            + coef[3, e][None] * after
            + coef[4, e][None] * turned(now, 1)
            + coef[5, e][None] * turned(now, Z - 1)
        )

    def sweep(level, e0, n):
        for m in range(3):
            part = pl.ds(8 * m, 8)
            before = u[level - 2][e0 - 1, part]
            now = u[level - 2][e0, part]
            for k in range(n):
                after = u[level - 2][e0 + k + 1, part]
                u[level - 1][e0 + k, part] = update(level, e0 + k, m, before, now, after)
                before, now = now, after

    def last_modes(e, count):
        result = []
        for m in range(count):
            part = pl.ds(8 * m, 8)
            result.append(update(8, e, m, u6[e - 1, part], u6[e, part], u6[e + 1, part]))
        return result

    def emit(e, slot):
        total, first, second = last_modes(e, 3)
        values = (total + first, total + second, total - first - second)
        for n, value in enumerate(values):
            spread[slot, pl.ds(n, K, stride=3), :] = value.reshape(K, Z)
        out[e - 8] = spread[slot].astype(jnp.bfloat16)

    for copy in own_cells:
        copy.wait()
    for e0 in (9, 17, 25, 31):
        coefficients(e0)
    own_f.wait()

    def pair_first(i, carry):
        first_level(9 + 2 * i, 0)
        first_level(10 + 2 * i, 1)
        return carry

    lax.fori_loop(0, 15, pair_first, 0)
    def rise(level, e0, n):
        def pair(i, carry):
            sweep(level, e0 + 2 * i, 2)
            return carry

        lax.fori_loop(0, n // 2, pair, 0)

    for level in range(2, 8):
        rise(level, 8 + level, 32 - 2 * level)

    def finish(copies):
        for copy in copies:
            copy.wait_recv()

    finish(r1)
    r2 = stage2(rows, r_send, r_recv)
    start(r2)

    finish(to_left)
    coefficients(39)

    def right_first(i, carry):
        first_level(39 + 2 * i, 0)
        first_level(40 + 2 * i, 1)
        return carry

    lax.fori_loop(0, 4, right_first, 0)

    for level in range(2, 8):
        rise(level, 40 - level, 8)
    total, first = last_modes(7 + ROWS, 2)
    traces[place] = (total + first).reshape(K, Z).astype(jnp.bfloat16)
    finish(r2)
    r3 = stage3(rows, r_send, r_recv)
    start(r3)
    t1 = stage1(traces, t_send, t_recv)
    start(t1)

    finish(to_right)
    coefficients(1)

    def left_first(i, carry):
        first_level(1 + 2 * i, 0)
        first_level(2 + 2 * i, 1)
        return carry

    lax.fori_loop(0, 4, left_first, 0)

    for level in range(2, 8):
        rise(level, level, 8)

    finish(t1)
    t2 = stage2(traces, t_send, t_recv)
    start(t2)
    finish(r3)
    rp = remote(rows.at[pl.ds(c * 64, 64)], rows.at[pl.ds(c * 64, 64)], rp_send, rp_recv, other)
    rp.start()

    def pair_emit(i, carry):
        emit(8 + 2 * i, 0)
        emit(9 + 2 * i, 1)
        return carry

    half = ROWS // 2
    lax.fori_loop(0, half // 2, pair_emit, 0)
    out0 = pltpu.make_async_copy(out.at[pl.ds(0, half)], basis_hbm.at[pl.ds(0, half)], out_sem.at[0])
    out0.start()

    finish(t2)
    t3 = stage3(traces, t_send, t_recv)
    start(t3)

    def slab(k):
        where = pl.ds(c * 64 + (a + 4 - k) % 4 * 16, 16)
        return remote(traces.at[where], traces.at[where], tp_send.at[k], tp_recv.at[k], other)

    tp = [slab(k) for k in range(4)]
    tp[0].start()

    lax.fori_loop(half // 2, half, pair_emit, 0)
    out1 = pltpu.make_async_copy(out.at[pl.ds(half, half)], basis_hbm.at[pl.ds(half, half)], out_sem.at[1])
    out1.start()

    contract = (((1,), (1,)), ((), ()))

    def product(left_side, right_side):
        return lax.dot_general(left_side, right_side, contract, preferred_element_type=jnp.float32)

    for copy in own_p:
        copy.wait()
    scales_t[...] = scales[...].T
    weights[...] = coeffs[...].astype(jnp.bfloat16)
    wide[...] = jnp.zeros_like(wide)
    wide[:, 0:K] = coeffs[...]
    low = wide[...]
    weights2[0:quarter] = low.astype(jnp.bfloat16)
    weights2[quarter : 2 * quarter] = pltpu.roll(low, K, 1).astype(jnp.bfloat16)

    for n in (0, 2, 1):
        t3[n].wait_recv()
        tp[n + 1].start()
    rp.wait_recv()
    finish(tp)

    def pick(slot):
        return jnp.maximum(table[slot], 0)

    def blocks(n, forward, backward):
        for q in range(4):
            i = 4 * n + q
            where = position(i)
            scaled = (traces[where].astype(jnp.float32) * rows[where]).astype(jnp.bfloat16)
            pair = jnp.concatenate([traces[position(pick(2 * i))], traces[position(pick(2 * i + 1))]], axis=0)
            forward[K * q : K * q + K] = product(scaled, pair).astype(jnp.bfloat16)
            backward[2 * K * q : 2 * K * q + 2 * K] = product(pair, scaled).astype(jnp.bfloat16)

    def residuals(n, forward, backward):
        ahead = product(forward[...], weights2[...])
        behind = product(backward[...], weights[...])
        for q in range(4):
            i = 4 * n + q
            own = scales_t[pl.ds(i, 1), :]
            for k in range(2):
                slot = 2 * i + k
                beside = scales_t[pl.ds(pick(slot), 1), :]
                residual = (
                    own * ahead[K * q : K * q + K, quarter * k : quarter * k + quarter]
                    - beside * behind[2 * K * q + K * k : 2 * K * q + K * k + K]
                )
                part = jnp.sum((residual * residual).reshape(8, 8, quarter), axis=0)
                parts[pl.ds(pl.multiple_of(8 * slot, 8), 8), :] = jnp.where(table[slot] >= 0, part, 0.0)

    chunks = traces.shape[0] // 4
    blocks(0, fw0, bw0)

    def two(i, carry):
        blocks(2 * i + 1, fw1, bw1)
        residuals(2 * i, fw0, bw0)
        blocks(jnp.minimum(2 * i + 2, chunks - 1), fw0, bw0)
        residuals(2 * i + 1, fw1, bw1)
        return carry

    lax.fori_loop(0, chunks // 2, two, 0)
    slots = norms.shape[1]
    squares = parts[pl.ds(0, slots, stride=8), :]
    for n in range(1, 8):
        squares = squares + parts[pl.ds(n, slots, stride=8), :]
    inbox[p] = jnp.sum(squares, axis=0, keepdims=True)
    norms[...] = jnp.sqrt(squares.T + EPS)
    shares = [
        remote(inbox.at[p], inbox.at[p], s_send.at[d - 1], s_recv.at[d - 1], (x, (p + d) % npatch))
        for d in range(1, npatch)
    ]
    start(shares)
    finish(shares)
    total = inbox[0]
    for n in range(1, npatch):
        total = total + inbox[n]
    estimate[...] = jnp.sqrt(total + EPS)
    for copy in to_left + to_right + r1 + r2 + r3 + [rp] + t1 + t2 + t3 + tp + shares:
        copy.wait_send()
    for copy in (out0, out1):
        copy.wait()


def owned(owner_map, adjacency, owner):
    mine = owner_map == owner
    earlier = jnp.pad(mine, ((0, 0), (1, 0)))[:, :-1]
    picked = jnp.stack([mine & ~earlier, mine & earlier], axis=1)
    found = jnp.sum(jnp.where(picked, adjacency[:, None, :] + 1, 0), axis=2)
    return (found - 1).reshape(-1)


def body(forcing, stiffness, reaction, volumetric, adjacency, owner_map, param_scale, coefficients):
    anywhere = pl.BlockSpec(memory_space=pl.ANY)
    vmem = pl.BlockSpec(memory_space=pltpu.VMEM)
    dma = pltpu.SemaphoreType.DMA
    f32, bf16 = jnp.float32, jnp.bfloat16
    table = owned(owner_map, adjacency, lax.axis_index("patch"))
    slots = table.shape[0]
    quarter = param_scale.shape[0] // lax.axis_size("grp")
    npatch = lax.axis_size("patch")
    basis, norms, estimate = pl.pallas_call(
        round_kernel,
        name="round",
        out_shape=(
            jax.ShapeDtypeStruct((ROWS, 3 * K, Z), bf16),
            jax.ShapeDtypeStruct((quarter, slots), f32),
            jax.ShapeDtypeStruct((1, quarter), f32),
        ),
        in_specs=[pl.BlockSpec(memory_space=pltpu.SMEM)] + [anywhere] * 6,
        out_specs=(anywhere, vmem, vmem),
        scratch_shapes=[pltpu.VMEM((48, 24, 8, Z), f32)] * 7
        + [
            pltpu.VMEM((48, 3 * K, Z), bf16),
            pltpu.VMEM((3, 48, Z), f32),
            pltpu.VMEM((7, 8, Z), f32),
            pltpu.VMEM((7, 48, 8, Z), f32),
            pltpu.VMEM((2, 3 * K, Z), f32),
            pltpu.VMEM((ROWS, 3 * K, Z), bf16),
            pltpu.VMEM((128, K, Z), bf16),
            pltpu.VMEM((128, 1, Z), f32),
            pltpu.VMEM((quarter, K), f32),
            pltpu.VMEM((quarter, 128), f32),
            pltpu.VMEM((128, quarter), f32),
            pltpu.VMEM((quarter, 2 * K), f32),
            pltpu.VMEM((quarter, K), bf16),
            pltpu.VMEM((2 * quarter, 2 * K), bf16),
            pltpu.VMEM((4 * K, 2 * K), bf16),
            pltpu.VMEM((8 * K, K), bf16),
            pltpu.VMEM((4 * K, 2 * K), bf16),
            pltpu.VMEM((8 * K, K), bf16),
            pltpu.VMEM((8 * slots, quarter), f32),
            pltpu.VMEM((npatch, 1, quarter), f32),
            dma((7,)),
            dma((2, 4)),
            dma((2, 4)),
            dma((3, 3)),
            dma((3, 3)),
            dma((3, 3)),
            dma((3, 3)),
            dma((4,)),
            dma((4,)),
            dma,
            dma,
            dma((2,)),
            dma((npatch - 1,)),
            dma((npatch - 1,)),
        ],
        compiler_params=pltpu.CompilerParams(collective_id=0, has_side_effects=True, vmem_limit_bytes=VMEM_LIMIT),
    )(table, forcing[0], stiffness[0], reaction[0], volumetric[0], coefficients, param_scale)
    return (basis[None], norms[None], estimate[0])


def solution(mesh):
    placed = (
        P("grp", "patch", None, None),
        P("grp", "patch", None),
        P("grp", "patch", None),
        P("grp", "patch", None),
        P(),
        P(),
        P(),
        P(),
    )
    return jax.shard_map(
        body,
        mesh=mesh,
        in_specs=placed,
        out_specs=(P("grp", "patch", None, None), P("patch", "grp", None), P("grp")),
        check_vma=False,
    )
```

time: 124 us -> 69.6 us (0.56)
  Pallas kernels: 119 us -> 60.7 us
  local copies, waits for them, and re-layouts: 2.79 us -> 6.43 us
    pallas_call x3 -> x1, Pallas kernels: 119 us -> 60.7 us  [body(): pl.pallas_call(round_kernel, name='round', out_shape=(jax.ShapeDtypeStruc...]
    unnamed x10 -> x8, local copies, waits for them, and re-layouts: 1.99 us -> 5.6 us
where the time goes in v1:
time: 69.6 us; the launch traced here: 69.3 us
  Pallas kernels  60.7 us (87%)
  local copies, waits for them, and re-layouts  6.43 us (9%)
  other arithmetic  1.5 us (2%)
    pallas_call x1, Pallas kernels, body(): pl.pallas_call(round_kernel, name='round', out_shape=(jax.ShapeDtypeStruc...  60.7 us
    unnamed x8, local copies, waits for them, and re-layouts  5.6 us

profile of v1, /device:TPU:1, one launch (start us, length us, event | category | flops | bytes accessed | tf_op | source)
XLA Modules:
  0.0 69.3 jit_solution(16852489666556028082)
XLA Ops:
  0.6 0.7 %broadcast_compare_fusion = pred[128,26]{0,1:T(8,128)(4,1)S(1)} fusion(s32[128,26]{0,1:T(8,128)} %param.13, s32[]{:T(128)S(6)} %axis_index.12), kind=kLoop, calls=%fused_computation.5 | loop fusion | flops 3328 | bytes 16644 | tf_op jit(solution)/shard_map/eq | solution.py:380
  1.4 0.7 %broadcast_add_fusion = s32[128,26]{0,1:T(8,128)S(1)} fusion(s32[128,26]{0,1:T(8,128)} %param.12), kind=kLoop, calls=%fused_computation.4 | loop fusion | flops 3328 | bytes 26624 | tf_op jit(solution)/shard_map/add | solution.py:383
  2.1 0.1 copy.13
  2.2 0.7 %sub.7.table = s32[256]{0:T(256)} reshape(s32[128,2]{1,0:T(8,128)S(1)} %copy.13) | data formatting | bytes 2048 | tf_op jit(solution)/shard_map/sub | solution.py:384
  3.0 1.7 %copy.14.coeffs_hbm = f32[512,64]{1,0:T(8,128)} copy(f32[512,64]{0,1:T(8,128)} %param.15) | data formatting | bytes 262144 | tf_op args[7]
  4.7 60.7 %round.1 = (bf16[32,192,128]{2,1,0:T(8,128)(2,1)}, f32[128,256]{1,0:T(8,128)}, f32[1,128]{1,0:T(1,128)}) custom-call(s32[256]{0:T(256)} %sub.7.table, bf16[32,192,128]{2,1,0:T(8,128)(2,1)} %bitcast.12, f32[32,128]{1,0:T(8,128)} %bitcast.14, f32[32,128]{1,0:T(8,128)} %bitcast.15, f32[32,128]{1,0:T(8,128)} %bitcast.16, f32[512,64]{1,0:T(8,128)} %copy.14.coeffs_hbm, ...), custom_call_target="tpu_custom_call" | custom-call | tf_op jit(solution)/shard_map/round/pallas_call | solution.py:396
  65.4 0.0 copy-start
  65.4 0.0 copy-start.1
  65.4 2.7 %copy.18 = bf16[1,32,192,128]{3,2,1,0:T(8,128)(2,1)} copy(bf16[1,32,192,128]{3,2,1,0:T(8,128)(2,1)} %bitcast.11) | data formatting | bytes 3145728
  68.1 0.0 copy-done
  68.1 0.7 copy.19
  68.8 0.0 copy-done.1
  68.8 0.5 copy.20
  (3 shorter events, 0.0 us)
Async XLA Ops:
  65.4 2.7 %copy-start = (f32[128,256]{1,0:T(8,128)S(1)}, f32[128,256]{1,0:T(8,128)}, u32[]{:S(2)}) copy-start(f32[128,256]{1,0:T(8,128)} %get-tuple-element.7) | copy-start | bytes 393220
  65.4 3.4 %copy-start.1 = (f32[1,128]{1,0:T(1,128)S(1)}, f32[1,128]{1,0:T(1,128)}, u32[]{:S(2)}) copy-start(f32[1,128]{1,0:T(1,128)} %get-tuple-element.8) | copy-start | bytes 1540

commit v2 on v1

--- a/solution.py
+++ b/solution.py
@@ -26,11 +26,11 @@
 
 
 def round_kernel(
-    table, f_hbm, s_hbm, r_hbm, v_hbm, coeffs_hbm, scales_hbm,
+    f_hbm, s_hbm, r_hbm, v_hbm, coeffs_hbm, scales_hbm, owners_hbm, adjacent_hbm,
     basis_hbm, norms, estimate,
     u0, u1, u2, u3, u4, u5, u6,
     fext, cells, small, coef, spread, out, traces, rows,
-    coeffs, scales, scales_t, wide, weights, weights2, fw0, bw0, fw1, bw1, parts, inbox,
+    owners, adjacent, found, table, shuffle, split, coeffs, scales, scales_t, weights, weights2, fw0, bw0, fw1, bw1, parts, inbox,
     local_sem, halo_send, halo_recv, t_send, t_recv, r_send, r_recv, tp_send, tp_recv, rp_send, rp_recv, out_sem,
     s_send, s_recv,
 ):
@@ -66,16 +66,40 @@
     own_row = pltpu.make_async_copy(s_hbm.at[pl.ds(ROWS - 1, 1)], rows.at[place], local_sem.at[4])
     quarter = norms.shape[0]
     own_p = [
-        pltpu.make_async_copy(coeffs_hbm.at[pl.ds(x * quarter, quarter)], coeffs, local_sem.at[5]),
+        pltpu.make_async_copy(coeffs_hbm.at[:, pl.ds(x * quarter, quarter)], coeffs, local_sem.at[5]),
         pltpu.make_async_copy(scales_hbm.at[pl.ds(x * quarter, quarter)], scales, local_sem.at[6]),
     ]
-    for copy in own_cells + [own_f, own_row] + own_p:
+    own_t = [
+        pltpu.make_async_copy(owners_hbm, owners, local_sem.at[7]),
+        pltpu.make_async_copy(adjacent_hbm, adjacent, local_sem.at[8]),
+    ]
+    for copy in own_cells + [own_f, own_row] + own_t + own_p:
         copy.start()
 
     barrier = pltpu.get_barrier_semaphore()
     peers = [(x, left), (x, right)] + firsts + grps + lasts + [other]
     for peer in peers:
         pl.semaphore_signal(barrier, inc=1, device_id=peer, device_id_type=MESH)
+
+    side = lax.broadcasted_iota(jnp.int32, (2 * Z, 2 * Z), 0)
+    lanes = lax.broadcasted_iota(jnp.int32, (2 * Z, 2 * Z), 1)
+    cell = 2 * (lanes & 63) + (lanes >> 7)
+    same_cell = (side & 127) == cell
+    shuffle[...] = jnp.where(same_cell & ((side >> 7) == ((lanes >> 6) & 1)), 1.0, 0.0).astype(jnp.bfloat16)
+    split[...] = jnp.where(same_cell[0:Z], 1.0, 0.0)
+    for copy in own_t:
+        copy.wait()
+    found[...] = jnp.zeros_like(found)
+    count = jnp.zeros((1, Z), jnp.int32)
+    picked = [count, count]
+    for n in range(owners.shape[0]):
+        mine = jnp.where(owners[pl.ds(n, 1), :] == p, 1, 0)
+        entry = adjacent[pl.ds(n, 1), :] + 1
+        for k in range(2):
+            picked[k] = picked[k] + jnp.where(count == k, mine * entry, 0)
+        count = count + mine
+    for k in range(2):
+        found[pl.ds(k, 1), :] = picked[k] - 1
     pl.semaphore_wait(barrier, len(peers))
 
     def remote(src, dst, ssem, rsem, device):
@@ -146,58 +170,97 @@
             weight * north * keep_n,
             weight * (1.0 / 3.0),
         )
-        for n, value in enumerate(values):
-            small[n] = value
+        parted = lax.dot_general(
+            jnp.concatenate(values, axis=0), split[...], (((1,), (0,)), ((), ())),
+            precision=lax.Precision.HIGHEST, preferred_element_type=jnp.float32,
+        )
+        small[...] = parted
         for n in range(7):
-            for k in range(8):
-                coef[n, e0 + k] = jnp.broadcast_to(small[n, pl.ds(k, 1), :], (8, Z))
+            for parity in range(2):
+                kind = 9 - n if n in (4, 5) and parity == 0 else n
+                for k in range(8):
+                    row = small[pl.ds(8 * n + k, 1), Z * parity : Z * parity + Z]
+                    coef[kind, e0 + k, parity] = jnp.broadcast_to(row, (8, Z))
+
+    half = 3 * K // 2
+    plain = (((1,), (0,)), ((), ()))
+    contract = (((1,), (1,)), ((), ()))
+
+    def product(left_side, right_side, dims=contract):
+        return lax.dot_general(left_side, right_side, dims, preferred_element_type=jnp.float32)
+
+    def block(m, parity):
+        return pl.ds(8 * m + 4 * parity, 4)
 
     def first_level(e, slot):
-        spread[slot] = fext[e].astype(jnp.float32)
-        parts = [spread[slot, pl.ds(n, K, stride=3), :].reshape(8, 8, Z) for n in range(3)]
-        weight = coef[6, e][None]
-        total = parts[0] + parts[1] + parts[2]
-        u0[e, 0:8] = weight * total
-        u0[e, 8:16] = weight * (3.0 * parts[0] - total)
-        u0[e, 16:24] = weight * (3.0 * parts[1] - total)
+        value = fext[e]
+        parted = product(jnp.concatenate([value[0:half], value[half:]], axis=1), shuffle[...], plain)
+        for parity in range(2):
+            spread[slot, parity] = parted[:, Z * parity : Z * parity + Z]
+        for parity in range(2):
+            parts = [spread[slot, parity, pl.ds(n, K // 2, stride=3), :].reshape(4, 8, Z) for n in range(3)]
+            weight = coef[6, e, parity][None]
+            total = parts[0] + parts[1] + parts[2]
+            u0[e, block(0, parity)] = weight * total
+            u0[e, block(1, parity)] = weight * (3.0 * parts[0] - total)
+            u0[e, block(2, parity)] = weight * (3.0 * parts[1] - total)
+
+    def first_levels(e0, n):
+        def four(i, carry):
+            for k in range(4):
+                first_level(e0 + 4 * i + k, k)
+            return carry
+
+        lax.fori_loop(0, n // 4, four, 0)
 
     def turned(value, shift):
-        return pltpu.roll(value.reshape(K, Z), shift, 1).reshape(8, 8, Z)
-
-    def update(level, e, m, before, now, after):
-        centre = coef[1 if m == 0 else 0, e][None]
+        return pltpu.roll(value.reshape(K // 2, Z), shift, 1).reshape(4, 8, Z)
+
+    def update(e, m, parity, before, now, after, beside):
+        centre = coef[1 if m == 0 else 0, e, parity][None]
         return (
-            u0[e, pl.ds(8 * m, 8)]
-            + centre * now
-            + coef[2, e][None] * before
-            + coef[3, e][None] * after
-            + coef[4, e][None] * turned(now, 1)
-            + coef[5, e][None] * turned(now, Z - 1)
+            u0[e, block(m, parity)]
+            + coef[2, e, parity][None] * before
+            + coef[3, e, parity][None] * after
+        ) + (
+            centre * now
+            + (coef[4, e, parity][None] * beside + coef[5, e, parity][None] * turned(beside, 1 if parity == 0 else Z - 1))
         )
 
     def sweep(level, e0, n):
+        below, mine = u[level - 2], u[level - 1]
         for m in range(3):
-            part = pl.ds(8 * m, 8)
-            before = u[level - 2][e0 - 1, part]
-            now = u[level - 2][e0, part]
-            for k in range(n):
-                after = u[level - 2][e0 + k + 1, part]
-                u[level - 1][e0 + k, part] = update(level, e0 + k, m, before, now, after)
-                before, now = now, after
+            for parity in range(2):
+                part = block(m, parity)
+                before = below[e0 - 1, part]
+                now = below[e0, part]
+                for k in range(n):
+                    after = below[e0 + k + 1, part]
+                    beside = below[e0 + k, block(m, 1 - parity)]
+                    mine[e0 + k, part] = update(e0 + k, m, parity, before, now, after, beside)
+                    before, now = now, after
 
     def last_modes(e, count):
         result = []
         for m in range(count):
-            part = pl.ds(8 * m, 8)
-            result.append(update(8, e, m, u6[e - 1, part], u6[e, part], u6[e + 1, part]))
+            both = []
+            for parity in range(2):
+                part = block(m, parity)
+                beside = u6[e, block(m, 1 - parity)]
+                both.append(update(e, m, parity, u6[e - 1, part], u6[e, part], u6[e + 1, part], beside))
+            result.append(both)
         return result
 
     def emit(e, slot):
         total, first, second = last_modes(e, 3)
-        values = (total + first, total + second, total - first - second)
-        for n, value in enumerate(values):
-            spread[slot, pl.ds(n, K, stride=3), :] = value.reshape(K, Z)
-        out[e - 8] = spread[slot].astype(jnp.bfloat16)
+        for parity in range(2):
+            t, f, g = total[parity], first[parity], second[parity]
+            for n, value in enumerate((t + f, t + g, t - f - g)):
+                spread[slot, parity, pl.ds(n, K // 2, stride=3), :] = value.reshape(K // 2, Z)
+        value = jnp.concatenate([spread[slot, 0], spread[slot, 1]], axis=1).astype(jnp.bfloat16)
+        joined = product(value, shuffle[...]).astype(jnp.bfloat16)
+        out[e - 8, 0:half] = joined[:, 0:Z]
+        out[e - 8, half:] = joined[:, Z:]
 
     for copy in own_cells:
         copy.wait()
@@ -205,21 +268,17 @@
         coefficients(e0)
     own_f.wait()
 
-    def pair_first(i, carry):
-        first_level(9 + 2 * i, 0)
-        first_level(10 + 2 * i, 1)
-        return carry
-
-    lax.fori_loop(0, 15, pair_first, 0)
-    def rise(level, e0, n):
-        def pair(i, carry):
-            sweep(level, e0 + 2 * i, 2)
+    first_levels(8, ROWS)
+    for level in range(2, 8):
+        eights, fours = divmod((32 - 2 * level + 3) // 4, 2)
+
+        def eight(i, carry, level=level):
+            sweep(level, 8 + level + 8 * i, 8)
             return carry
 
-        lax.fori_loop(0, n // 2, pair, 0)
-
-    for level in range(2, 8):
-        rise(level, 8 + level, 32 - 2 * level)
+        lax.fori_loop(0, eights, eight, 0)
+        if fours:
+            sweep(level, 8 + level + 8 * eights, 4)
 
     def finish(copies):
         for copy in copies:
@@ -232,17 +291,14 @@
     finish(to_left)
     coefficients(39)
 
-    def right_first(i, carry):
-        first_level(39 + 2 * i, 0)
-        first_level(40 + 2 * i, 1)
-        return carry
-
-    lax.fori_loop(0, 4, right_first, 0)
-
+    first_levels(39, 8)
     for level in range(2, 8):
-        rise(level, 40 - level, 8)
+        sweep(level, 40 - level, 8)
     total, first = last_modes(7 + ROWS, 2)
-    traces[place] = (total + first).reshape(K, Z).astype(jnp.bfloat16)
+    ends = [(total[parity] + first[parity]).reshape(K // 2, Z).astype(jnp.bfloat16) for parity in range(2)]
+    trace = product(jnp.concatenate(ends, axis=1), shuffle[...]).astype(jnp.bfloat16)
+    traces[place, 0 : K // 2] = trace[:, 0:Z]
+    traces[place, K // 2 :] = trace[:, Z:]
     finish(r2)
     r3 = stage3(rows, r_send, r_recv)
     start(r3)
@@ -252,15 +308,9 @@
     finish(to_right)
     coefficients(1)
 
-    def left_first(i, carry):
-        first_level(1 + 2 * i, 0)
-        first_level(2 + 2 * i, 1)
-        return carry
-
-    lax.fori_loop(0, 4, left_first, 0)
-
+    first_levels(1, 8)
     for level in range(2, 8):
-        rise(level, level, 8)
+        sweep(level, level, 8)
 
     finish(t1)
     t2 = stage2(traces, t_send, t_recv)
@@ -269,14 +319,14 @@
     rp = remote(rows.at[pl.ds(c * 64, 64)], rows.at[pl.ds(c * 64, 64)], rp_send, rp_recv, other)
     rp.start()
 
-    def pair_emit(i, carry):
-        emit(8 + 2 * i, 0)
-        emit(9 + 2 * i, 1)
+    def four_emit(i, carry):
+        for k in range(4):
+            emit(8 + 4 * i + k, k)
         return carry
 
-    half = ROWS // 2
-    lax.fori_loop(0, half // 2, pair_emit, 0)
-    out0 = pltpu.make_async_copy(out.at[pl.ds(0, half)], basis_hbm.at[pl.ds(0, half)], out_sem.at[0])
+    middle = ROWS // 2
+    lax.fori_loop(0, middle // 4, four_emit, 0)
+    out0 = pltpu.make_async_copy(out.at[pl.ds(0, middle)], basis_hbm.at[pl.ds(0, middle)], out_sem.at[0])
     out0.start()
 
     finish(t2)
@@ -290,24 +340,21 @@
     tp = [slab(k) for k in range(4)]
     tp[0].start()
 
-    lax.fori_loop(half // 2, half, pair_emit, 0)
-    out1 = pltpu.make_async_copy(out.at[pl.ds(half, half)], basis_hbm.at[pl.ds(half, half)], out_sem.at[1])
+    lax.fori_loop(middle // 4, ROWS // 4, four_emit, 0)
+    out1 = pltpu.make_async_copy(out.at[pl.ds(middle, middle)], basis_hbm.at[pl.ds(middle, middle)], out_sem.at[1])
     out1.start()
 
-    contract = (((1,), (1,)), ((), ()))
-
-    def product(left_side, right_side):
-        return lax.dot_general(left_side, right_side, contract, preferred_element_type=jnp.float32)
-
+    to_table = pltpu.make_async_copy(found, table, local_sem.at[9])
+    to_table.start()
     for copy in own_p:
         copy.wait()
     scales_t[...] = scales[...].T
-    weights[...] = coeffs[...].astype(jnp.bfloat16)
-    wide[...] = jnp.zeros_like(wide)
-    wide[:, 0:K] = coeffs[...]
-    low = wide[...]
-    weights2[0:quarter] = low.astype(jnp.bfloat16)
-    weights2[quarter : 2 * quarter] = pltpu.roll(low, K, 1).astype(jnp.bfloat16)
+    narrow = coeffs[...].astype(jnp.bfloat16)
+    weights[...] = narrow
+    weights2[...] = jnp.zeros_like(weights2)
+    weights2[0:K, 0:quarter] = narrow
+    weights2[K:, quarter:] = narrow
+    to_table.wait()
 
     for n in (0, 2, 1):
         t3[n].wait_recv()
@@ -315,33 +362,33 @@
     rp.wait_recv()
     finish(tp)
 
-    def pick(slot):
-        return jnp.maximum(table[slot], 0)
+    def pick(i, k):
+        return jnp.maximum(table[k, i], 0)
 
     def blocks(n, forward, backward):
         for q in range(4):
             i = 4 * n + q
             where = position(i)
             scaled = (traces[where].astype(jnp.float32) * rows[where]).astype(jnp.bfloat16)
-            pair = jnp.concatenate([traces[position(pick(2 * i))], traces[position(pick(2 * i + 1))]], axis=0)
+            pair = jnp.concatenate([traces[position(pick(i, 0))], traces[position(pick(i, 1))]], axis=0)
             forward[K * q : K * q + K] = product(scaled, pair).astype(jnp.bfloat16)
             backward[2 * K * q : 2 * K * q + 2 * K] = product(pair, scaled).astype(jnp.bfloat16)
 
     def residuals(n, forward, backward):
-        ahead = product(forward[...], weights2[...])
-        behind = product(backward[...], weights[...])
+        ahead = product(forward[...], weights2[...], plain)
+        behind = product(backward[...], weights[...], plain)
         for q in range(4):
             i = 4 * n + q
             own = scales_t[pl.ds(i, 1), :]
             for k in range(2):
                 slot = 2 * i + k
-                beside = scales_t[pl.ds(pick(slot), 1), :]
+                beside = scales_t[pl.ds(pick(i, k), 1), :]
                 residual = (
                     own * ahead[K * q : K * q + K, quarter * k : quarter * k + quarter]
                     - beside * behind[2 * K * q + K * k : 2 * K * q + K * k + K]
                 )
                 part = jnp.sum((residual * residual).reshape(8, 8, quarter), axis=0)
-                parts[pl.ds(pl.multiple_of(8 * slot, 8), 8), :] = jnp.where(table[slot] >= 0, part, 0.0)
+                parts[pl.ds(pl.multiple_of(8 * slot, 8), 8), :] = jnp.where(table[k, i] >= 0, part, 0.0)
 
     chunks = traces.shape[0] // 4
     blocks(0, fw0, bw0)
@@ -376,21 +423,12 @@
         copy.wait()
 
 
-def owned(owner_map, adjacency, owner):
-    mine = owner_map == owner
-    earlier = jnp.pad(mine, ((0, 0), (1, 0)))[:, :-1]
-    picked = jnp.stack([mine & ~earlier, mine & earlier], axis=1)
-    found = jnp.sum(jnp.where(picked, adjacency[:, None, :] + 1, 0), axis=2)
-    return (found - 1).reshape(-1)
-
-
 def body(forcing, stiffness, reaction, volumetric, adjacency, owner_map, param_scale, coefficients):
     anywhere = pl.BlockSpec(memory_space=pl.ANY)
     vmem = pl.BlockSpec(memory_space=pltpu.VMEM)
     dma = pltpu.SemaphoreType.DMA
     f32, bf16 = jnp.float32, jnp.bfloat16
-    table = owned(owner_map, adjacency, lax.axis_index("patch"))
-    slots = table.shape[0]
+    slots = 2 * owner_map.shape[0]
     quarter = param_scale.shape[0] // lax.axis_size("grp")
     npatch = lax.axis_size("patch")
     basis, norms, estimate = pl.pallas_call(
@@ -401,31 +439,36 @@
             jax.ShapeDtypeStruct((quarter, slots), f32),
             jax.ShapeDtypeStruct((1, quarter), f32),
         ),
-        in_specs=[pl.BlockSpec(memory_space=pltpu.SMEM)] + [anywhere] * 6,
+        in_specs=[anywhere] * 8,
         out_specs=(anywhere, vmem, vmem),
         scratch_shapes=[pltpu.VMEM((48, 24, 8, Z), f32)] * 7
         + [
             pltpu.VMEM((48, 3 * K, Z), bf16),
             pltpu.VMEM((3, 48, Z), f32),
-            pltpu.VMEM((7, 8, Z), f32),
-            pltpu.VMEM((7, 48, 8, Z), f32),
-            pltpu.VMEM((2, 3 * K, Z), f32),
+            pltpu.VMEM((56, 2 * Z), f32),
+            pltpu.VMEM((7, 48, 2, 8, Z), f32),
+            pltpu.VMEM((4, 2, 3 * K // 2, Z), f32),
             pltpu.VMEM((ROWS, 3 * K, Z), bf16),
             pltpu.VMEM((128, K, Z), bf16),
             pltpu.VMEM((128, 1, Z), f32),
-            pltpu.VMEM((quarter, K), f32),
+            pltpu.VMEM(owner_map.T.shape, jnp.int32),
+            pltpu.VMEM(owner_map.T.shape, jnp.int32),
+            pltpu.VMEM((8, Z), jnp.int32),
+            pltpu.SMEM((8, Z), jnp.int32),
+            pltpu.VMEM((2 * Z, 2 * Z), bf16),
+            pltpu.VMEM((Z, 2 * Z), f32),
+            pltpu.VMEM((K, quarter), f32),
             pltpu.VMEM((quarter, 128), f32),
             pltpu.VMEM((128, quarter), f32),
-            pltpu.VMEM((quarter, 2 * K), f32),
-            pltpu.VMEM((quarter, K), bf16),
-            pltpu.VMEM((2 * quarter, 2 * K), bf16),
+            pltpu.VMEM((K, quarter), bf16),
+            pltpu.VMEM((2 * K, 2 * quarter), bf16),
             pltpu.VMEM((4 * K, 2 * K), bf16),
             pltpu.VMEM((8 * K, K), bf16),
             pltpu.VMEM((4 * K, 2 * K), bf16),
             pltpu.VMEM((8 * K, K), bf16),
             pltpu.VMEM((8 * slots, quarter), f32),
             pltpu.VMEM((npatch, 1, quarter), f32),
-            dma((7,)),
+            dma((10,)),
             dma((2, 4)),
             dma((2, 4)),
             dma((3, 3)),
@@ -441,7 +484,9 @@
             dma((npatch - 1,)),
         ],
         compiler_params=pltpu.CompilerParams(collective_id=0, has_side_effects=True, vmem_limit_bytes=VMEM_LIMIT),
-    )(table, forcing[0], stiffness[0], reaction[0], volumetric[0], coefficients, param_scale)
+    )(
+        forcing[0], stiffness[0], reaction[0], volumetric[0], coefficients.T, param_scale, owner_map.T, adjacency.T
+    )
     return (basis[None], norms[None], estimate[0])
 
 

time: 69.6 us -> 57.3 us (0.82)
  Pallas kernels: 60.7 us -> 52.6 us
  local copies, waits for them, and re-layouts: 6.43 us -> 3.87 us
  other arithmetic: 1.5 us -> 0 us
    pallas_call x1, Pallas kernels: 60.7 us -> 52.6 us  [body(): pl.pallas_call(round_kernel, name='round', out_shape=(jax.ShapeDtypeStruc...]
    unnamed x8 -> x7, local copies, waits for them, and re-layouts: 5.6 us -> 3.87 us
    sub x2 -> x0, local copies, waits for them, and re-layouts: 0.82 us -> none  [owned(): return (found - 1).reshape(-1)]
    eq x1 -> x0, other arithmetic: 0.72 us -> none  [owned(): mine = owner_map == owner]
    add x1 -> x0, other arithmetic: 0.72 us -> none  [owned(): found = jnp.sum(jnp.where(picked, adjacency[:, None, :] + 1, 0), axis=2)]
where the time goes in v2:
time: 57.3 us; the launch traced here: 57.2 us
  Pallas kernels  52.6 us (92%)
  local copies, waits for them, and re-layouts  3.87 us (7%)
  between operations  0.66 us (1%)
    pallas_call x1, Pallas kernels, body(): pl.pallas_call(round_kernel, name='round', out_shape=(jax.ShapeDtypeStruc...  52.6 us
    unnamed x7, local copies, waits for them, and re-layouts  3.87 us

profile of v2, /device:TPU:1, one launch (start us, length us, event | category | flops | bytes accessed | tf_op | source)
XLA Modules:
  0.0 57.2 jit_solution(15179025317219764517)
XLA Ops:
  0.6 52.6 %round.1 = (bf16[32,192,128]{2,1,0:T(8,128)(2,1)}, f32[128,256]{1,0:T(8,128)}, f32[1,128]{1,0:T(1,128)}) custom-call(bf16[32,192,128]{2,1,0:T(8,128)(2,1)} %bitcast.11, f32[32,128]{1,0:T(8,128)} %bitcast.14, f32[32,128]{1,0:T(8,128)} %bitcast.15, f32[32,128]{1,0:T(8,128)} %bitcast.16, f32[64,512]{1,0:T(8,128)} %bitcast.12, f32[512,128]{1,0:T(8,128)} %scales_hbm.1, ...), custom_call_target="tpu_custom_call" | custom-call | tf_op jit(solution)/shard_map/round/pallas_call | solution.py:434
  53.3 0.0 copy-start
  53.3 0.0 copy-start.1
  53.3 2.7 %copy.14 = bf16[1,32,192,128]{3,2,1,0:T(8,128)(2,1)} copy(bf16[1,32,192,128]{3,2,1,0:T(8,128)(2,1)} %bitcast.10) | data formatting | bytes 3145728
  56.0 0.0 copy-done
  56.0 0.7 %copy.15 = f32[1,128,256]{2,1,0:T(8,128)} copy(f32[1,128,256]{2,1,0:T(8,128)S(1)} %bitcast.13) | data formatting | bytes 262144
  56.6 0.0 copy-done.1
  56.6 0.5 copy.16
Async XLA Ops:
  53.3 2.7 %copy-start = (f32[128,256]{1,0:T(8,128)S(1)}, f32[128,256]{1,0:T(8,128)}, u32[]{:S(2)}) copy-start(f32[128,256]{1,0:T(8,128)} %get-tuple-element.7) | copy-start | bytes 393220
  53.3 3.4 %copy-start.1 = (f32[1,128]{1,0:T(1,128)S(1)}, f32[1,128]{1,0:T(1,128)}, u32[]{:S(2)}) copy-start(f32[1,128]{1,0:T(1,128)} %get-tuple-element.8) | copy-start | bytes 1540

commit v3 on v2

--- a/solution.py
+++ b/solution.py
@@ -20,9 +20,7 @@
     y = (i >> 1) & 3
     z = (i >> 3) & 3
     x = i >> 5
-    last = jnp.where(core == 0, z, y)
-    first = jnp.where(core == 0, y, z)
-    return core * 64 + last * 16 + x * 4 + first
+    return core * 64 + jnp.where(core == 0, z * 16 + x * 4 + y, x * 16 + y * 4 + z)
 
 
 def round_kernel(
@@ -31,7 +29,7 @@
     u0, u1, u2, u3, u4, u5, u6,
     fext, cells, small, coef, spread, out, traces, rows,
     owners, adjacent, found, table, shuffle, split, coeffs, scales, scales_t, weights, weights2, fw0, bw0, fw1, bw1, parts, inbox,
-    local_sem, halo_send, halo_recv, t_send, t_recv, r_send, r_recv, tp_send, tp_recv, rp_send, rp_recv, out_sem,
+    local_sem, halo_send, halo_recv, t_send, t_recv, r_send, r_recv, f_send, f_recv, tp_send, tp_recv, rp_send, rp_recv, out_sem,
     s_send, s_recv,
 ):
     x = lax.axis_index("grp")
@@ -39,23 +37,26 @@
     c = p % 2
     y = (p // 2) % 4
     z = p // 8
-    a = jnp.where(c == 0, z, y)
+    a = jnp.where(c == 0, z, x)
+    m = jnp.where(c == 0, x, y)
     b = jnp.where(c == 0, y, z)
     npatch = 32
     u = (u0, u1, u2, u3, u4, u5, u6)
     line = c * 64 + a * 16
-    plane = line + x * 4
+    plane = line + m * 4
     place = plane + b
     right = (p + 1) % npatch
     left = (p + npatch - 1) % npatch
     partner = p + 1 - 2 * c
 
-    def patch_of(last, first):
-        return last * (8 - 6 * c) + first * (2 + 6 * c) + c
-
-    firsts = [(x, patch_of(a, (b + d) % 4)) for d in (1, 2, 3)]
-    grps = [((x + d) % 4, p) for d in (1, 2, 3)]
-    lasts = [(x, patch_of((a + d) % 4, b)) for d in (1, 2, 3)]
+    def device(last, middle, first):
+        last, middle, first = last % 4, middle % 4, first % 4
+        far = jnp.where(c == 0, last, first) * 8 + jnp.where(c == 0, first, middle) * 2 + c
+        return (jnp.where(c == 0, middle, last), far)
+
+    firsts = [device(a, m, b + d) for d in (1, 2, 3)]
+    grps = [device(a, m + d, b) for d in (1, 2, 3)]
+    lasts = [device(a + d, m, b) for d in (1, 2, 3)]
     other = (x, partner)
 
     own_f = pltpu.make_async_copy(f_hbm, fext.at[pl.ds(8, ROWS)], local_sem.at[0])
@@ -315,6 +316,39 @@
     finish(t1)
     t2 = stage2(traces, t_send, t_recv)
     start(t2)
+
+    def part(back, k):
+        return traces.at[pl.ds(c * 64 + (a + 4 - back) % 4 * 16 + (m + k) % 4 * 4, 4)]
+
+    def share(back, k):
+        return remote(part(back, k), part(back, k), tp_send.at[back, k], tp_recv.at[back, k], other)
+
+    ahead_of = [remote(part(0, k), part(0, k), f_send.at[0, k], f_recv.at[0, k], lasts[0]) for k in range(4)]
+    behind_of = [remote(part(0, k), part(0, k), f_send.at[1, k], f_recv.at[1, k], lasts[2]) for k in range(4)]
+    relay = [
+        remote(part(1, k), part(1, k), f_send.at[2, k], f_recv.at[2, k], lasts[0])
+        if k % 2 == 0
+        else remote(part(3, k), part(3, k), f_send.at[2, k], f_recv.at[2, k], lasts[2])
+        for k in range(4)
+    ]
+    tp = [[share(back, k) for k in range(4)] for back in range(4)]
+
+    def spread_out(k):
+        ahead_of[k].start()
+        behind_of[k].start()
+        tp[0][k].start()
+
+    def pass_on(k):
+        ahead_of[k].wait_recv()
+        if k % 2 == 0:
+            relay[k].start()
+        behind_of[k].wait_recv()
+        if k % 2 == 1:
+            relay[k].start()
+        tp[1][k].start()
+        tp[3][k].start()
+
+    spread_out(0)
     finish(r3)
     rp = remote(rows.at[pl.ds(c * 64, 64)], rows.at[pl.ds(c * 64, 64)], rp_send, rp_recv, other)
     rp.start()
@@ -324,25 +358,28 @@
             emit(8 + 4 * i + k, k)
         return carry
 
-    middle = ROWS // 2
-    lax.fori_loop(0, middle // 4, four_emit, 0)
-    out0 = pltpu.make_async_copy(out.at[pl.ds(0, middle)], basis_hbm.at[pl.ds(0, middle)], out_sem.at[0])
-    out0.start()
-
-    finish(t2)
-    t3 = stage3(traces, t_send, t_recv)
-    start(t3)
-
-    def slab(k):
-        where = pl.ds(c * 64 + (a + 4 - k) % 4 * 16, 16)
-        return remote(traces.at[where], traces.at[where], tp_send.at[k], tp_recv.at[k], other)
-
-    tp = [slab(k) for k in range(4)]
-    tp[0].start()
-
-    lax.fori_loop(middle // 4, ROWS // 4, four_emit, 0)
-    out1 = pltpu.make_async_copy(out.at[pl.ds(middle, middle)], basis_hbm.at[pl.ds(middle, middle)], out_sem.at[1])
-    out1.start()
+    quarters = []
+
+    def emit_quarter(n):
+        lax.fori_loop(2 * n, 2 * n + 2, four_emit, 0)
+        rows_out = pl.ds(8 * n, 8)
+        copy = pltpu.make_async_copy(out.at[rows_out], basis_hbm.at[rows_out], out_sem.at[n])
+        copy.start()
+        quarters.append(copy)
+
+    emit_quarter(0)
+    emit_quarter(1)
+    for k in (1, 3):
+        t2[3 - k].wait_recv()
+        spread_out(k)
+    pass_on(0)
+    t2[1].wait_recv()
+    spread_out(2)
+    emit_quarter(2)
+    pass_on(1)
+    pass_on(3)
+    emit_quarter(3)
+    pass_on(2)
 
     to_table = pltpu.make_async_copy(found, table, local_sem.at[9])
     to_table.start()
@@ -356,11 +393,12 @@
     weights2[K:, quarter:] = narrow
     to_table.wait()
 
-    for n in (0, 2, 1):
-        t3[n].wait_recv()
-        tp[n + 1].start()
+    for k in (0, 1, 3, 2):
+        relay[k].wait_recv()
+        tp[2][k].start()
     rp.wait_recv()
-    finish(tp)
+    for copies in tp:
+        finish(copies)
 
     def pick(i, k):
         return jnp.maximum(table[k, i], 0)
@@ -417,9 +455,9 @@
     for n in range(1, npatch):
         total = total + inbox[n]
     estimate[...] = jnp.sqrt(total + EPS)
-    for copy in to_left + to_right + r1 + r2 + r3 + [rp] + t1 + t2 + t3 + tp + shares:
+    for copy in to_left + to_right + r1 + r2 + r3 + [rp] + t1 + t2 + ahead_of + behind_of + relay + sum(tp, []) + shares:
         copy.wait_send()
-    for copy in (out0, out1):
+    for copy in quarters:
         copy.wait()
 
 
@@ -475,11 +513,13 @@
             dma((3, 3)),
             dma((3, 3)),
             dma((3, 3)),
-            dma((4,)),
-            dma((4,)),
+            dma((3, 4)),
+            dma((3, 4)),
+            dma((4, 4)),
+            dma((4, 4)),
             dma,
             dma,
-            dma((2,)),
+            dma((4,)),
             dma((npatch - 1,)),
             dma((npatch - 1,)),
         ],

time: 57.3 us -> 57.2 us (level)
  no operation moved by 1% of the time
where the time goes in v3:
time: 57.2 us; the launch traced here: 57.1 us
  Pallas kernels  52.5 us (92%)
  local copies, waits for them, and re-layouts  3.87 us (7%)
  between operations  0.66 us (1%)
    pallas_call x1, Pallas kernels, body(): pl.pallas_call(round_kernel, name='round', out_shape=(jax.ShapeDtypeStruc...  52.5 us
    unnamed x7, local copies, waits for them, and re-layouts  3.87 us

profile of v3, /device:TPU:1, one launch (start us, length us, event | category | flops | bytes accessed | tf_op | source)
XLA Modules:
  0.0 57.1 jit_solution(267826930646906259)
XLA Ops:
  0.6 52.5 %round.1 = (bf16[32,192,128]{2,1,0:T(8,128)(2,1)}, f32[128,256]{1,0:T(8,128)}, f32[1,128]{1,0:T(1,128)}) custom-call(bf16[32,192,128]{2,1,0:T(8,128)(2,1)} %bitcast.11, f32[32,128]{1,0:T(8,128)} %bitcast.14, f32[32,128]{1,0:T(8,128)} %bitcast.15, f32[32,128]{1,0:T(8,128)} %bitcast.16, f32[64,512]{1,0:T(8,128)} %bitcast.12, f32[512,128]{1,0:T(8,128)} %scales_hbm.1, ...), custom_call_target="tpu_custom_call" | custom-call | tf_op jit(solution)/shard_map/round/pallas_call | solution.py:472
  53.2 0.0 copy-start
  53.2 0.0 copy-start.1
  53.2 2.7 %copy.14 = bf16[1,32,192,128]{3,2,1,0:T(8,128)(2,1)} copy(bf16[1,32,192,128]{3,2,1,0:T(8,128)(2,1)} %bitcast.10) | data formatting | bytes 3145728
  55.9 0.0 copy-done
  55.9 0.7 %copy.15 = f32[1,128,256]{2,1,0:T(8,128)} copy(f32[1,128,256]{2,1,0:T(8,128)S(1)} %bitcast.13) | data formatting | bytes 262144
  56.6 0.0 copy-done.1
  56.6 0.5 copy.16
Async XLA Ops:
  53.2 2.7 %copy-start = (f32[128,256]{1,0:T(8,128)S(1)}, f32[128,256]{1,0:T(8,128)}, u32[]{:S(2)}) copy-start(f32[128,256]{1,0:T(8,128)} %get-tuple-element.7) | copy-start | bytes 393220
  53.2 3.4 %copy-start.1 = (f32[1,128]{1,0:T(1,128)S(1)}, f32[1,128]{1,0:T(1,128)}, u32[]{:S(2)}) copy-start(f32[1,128]{1,0:T(1,128)} %get-tuple-element.8) | copy-start | bytes 1540

commit v4 on v3

--- a/solution.py
+++ b/solution.py
@@ -303,8 +303,15 @@
     finish(r2)
     r3 = stage3(rows, r_send, r_recv)
     start(r3)
-    t1 = stage1(traces, t_send, t_recv)
-    start(t1)
+    plane_of = {
+        (dm, db): remote(
+            traces.at[place], traces.at[place], t_send.at[dm, db], t_recv.at[dm, db], device(a, m + dm, b + db)
+        )
+        for dm in (2, 1, 3, 0)
+        for db in (2, 1, 3, 0)
+        if dm or db
+    }
+    start(plane_of.values())
 
     finish(to_right)
     coefficients(1)
@@ -313,10 +320,6 @@
     for level in range(2, 8):
         sweep(level, level, 8)
 
-    finish(t1)
-    t2 = stage2(traces, t_send, t_recv)
-    start(t2)
-
     def part(back, k):
         return traces.at[pl.ds(c * 64 + (a + 4 - back) % 4 * 16 + (m + k) % 4 * 4, 4)]
 
@@ -325,26 +328,31 @@
 
     ahead_of = [remote(part(0, k), part(0, k), f_send.at[0, k], f_recv.at[0, k], lasts[0]) for k in range(4)]
     behind_of = [remote(part(0, k), part(0, k), f_send.at[1, k], f_recv.at[1, k], lasts[2]) for k in range(4)]
-    relay = [
-        remote(part(1, k), part(1, k), f_send.at[2, k], f_recv.at[2, k], lasts[0])
-        if k % 2 == 0
-        else remote(part(3, k), part(3, k), f_send.at[2, k], f_recv.at[2, k], lasts[2])
-        for k in range(4)
+    twice = [
+        remote(part(1, 0), part(1, 0), f_send.at[2, 0], f_recv.at[2, 0], lasts[0]),
+        remote(part(3, 1), part(3, 1), f_send.at[2, 1], f_recv.at[2, 1], lasts[2]),
+        remote(part(0, 2), part(0, 2), f_send.at[2, 2], f_recv.at[2, 2], lasts[1]),
+        remote(part(0, 3), part(0, 3), f_send.at[2, 3], f_recv.at[2, 3], lasts[1]),
     ]
     tp = [[share(back, k) for k in range(4)] for back in range(4)]
 
     def spread_out(k):
+        for db in range(4):
+            if k or db:
+                plane_of[(4 - k) % 4, db].wait_recv()
+        if k >= 2:
+            twice[k].start()
         ahead_of[k].start()
         behind_of[k].start()
         tp[0][k].start()
 
     def pass_on(k):
         ahead_of[k].wait_recv()
-        if k % 2 == 0:
-            relay[k].start()
+        if k == 0:
+            twice[k].start()
         behind_of[k].wait_recv()
-        if k % 2 == 1:
-            relay[k].start()
+        if k == 1:
+            twice[k].start()
         tp[1][k].start()
         tp[3][k].start()
 
@@ -368,17 +376,15 @@
         quarters.append(copy)
 
     emit_quarter(0)
+    spread_out(1)
+    spread_out(3)
+    spread_out(2)
     emit_quarter(1)
-    for k in (1, 3):
-        t2[3 - k].wait_recv()
-        spread_out(k)
     pass_on(0)
-    t2[1].wait_recv()
-    spread_out(2)
     emit_quarter(2)
     pass_on(1)
+    emit_quarter(3)
     pass_on(3)
-    emit_quarter(3)
     pass_on(2)
 
     to_table = pltpu.make_async_copy(found, table, local_sem.at[9])
@@ -394,7 +400,7 @@
     to_table.wait()
 
     for k in (0, 1, 3, 2):
-        relay[k].wait_recv()
+        twice[k].wait_recv()
         tp[2][k].start()
     rp.wait_recv()
     for copies in tp:
@@ -455,7 +461,7 @@
     for n in range(1, npatch):
         total = total + inbox[n]
     estimate[...] = jnp.sqrt(total + EPS)
-    for copy in to_left + to_right + r1 + r2 + r3 + [rp] + t1 + t2 + ahead_of + behind_of + relay + sum(tp, []) + shares:
+    for copy in to_left + to_right + r1 + r2 + r3 + [rp] + list(plane_of.values()) + ahead_of + behind_of + twice + sum(tp, []) + shares:
         copy.wait_send()
     for copy in quarters:
         copy.wait()
@@ -509,8 +515,8 @@
             dma((10,)),
             dma((2, 4)),
             dma((2, 4)),
-            dma((3, 3)),
-            dma((3, 3)),
+            dma((4, 4)),
+            dma((4, 4)),
             dma((3, 3)),
             dma((3, 3)),
             dma((3, 4)),

time: 57.2 us -> 53.8 us (0.941)
  Pallas kernels: 52.5 us -> 49.1 us
    pallas_call x1, Pallas kernels: 52.5 us -> 49.1 us  [body(): pl.pallas_call(round_kernel, name='round', out_shape=(jax.ShapeDtypeStruc...]
where the time goes in v4:
time: 53.8 us; the launch traced here: 53.7 us
  Pallas kernels  49.1 us (91%)
  local copies, waits for them, and re-layouts  3.87 us (7%)
  between operations  0.66 us (1%)
    pallas_call x1, Pallas kernels, body(): pl.pallas_call(round_kernel, name='round', out_shape=(jax.ShapeDtypeStruc...  49.1 us
    unnamed x7, local copies, waits for them, and re-layouts  3.87 us

profile of v4, /device:TPU:1, one launch (start us, length us, event | category | flops | bytes accessed | tf_op | source)
XLA Modules:
  0.0 53.7 jit_solution(11770420726227377458)
XLA Ops:
  0.6 49.1 %round.1 = (bf16[32,192,128]{2,1,0:T(8,128)(2,1)}, f32[128,256]{1,0:T(8,128)}, f32[1,128]{1,0:T(1,128)}) custom-call(bf16[32,192,128]{2,1,0:T(8,128)(2,1)} %bitcast.11, f32[32,128]{1,0:T(8,128)} %bitcast.14, f32[32,128]{1,0:T(8,128)} %bitcast.15, f32[32,128]{1,0:T(8,128)} %bitcast.16, f32[64,512]{1,0:T(8,128)} %bitcast.12, f32[512,128]{1,0:T(8,128)} %scales_hbm.1, ...), custom_call_target="tpu_custom_call" | custom-call | tf_op jit(solution)/shard_map/round/pallas_call | solution.py:478
  49.8 0.0 copy-start
  49.8 0.0 copy-start.1
  49.8 2.7 %copy.14 = bf16[1,32,192,128]{3,2,1,0:T(8,128)(2,1)} copy(bf16[1,32,192,128]{3,2,1,0:T(8,128)(2,1)} %bitcast.10) | data formatting | bytes 3145728
  52.5 0.0 copy-done
  52.5 0.7 %copy.15 = f32[1,128,256]{2,1,0:T(8,128)} copy(f32[1,128,256]{2,1,0:T(8,128)S(1)} %bitcast.13) | data formatting | bytes 262144
  53.1 0.0 copy-done.1
  53.1 0.5 copy.16
Async XLA Ops:
  49.8 2.7 %copy-start = (f32[128,256]{1,0:T(8,128)S(1)}, f32[128,256]{1,0:T(8,128)}, u32[]{:S(2)}) copy-start(f32[128,256]{1,0:T(8,128)} %get-tuple-element.7) | copy-start | bytes 393220
  49.8 3.4 %copy-start.1 = (f32[1,128]{1,0:T(1,128)S(1)}, f32[1,128]{1,0:T(1,128)}, u32[]{:S(2)}) copy-start(f32[1,128]{1,0:T(1,128)} %get-tuple-element.8) | copy-start | bytes 1540

commit v5 on v4

--- a/solution.py
+++ b/solution.py
@@ -25,11 +25,11 @@
 
 def round_kernel(
     f_hbm, s_hbm, r_hbm, v_hbm, coeffs_hbm, scales_hbm, owners_hbm, adjacent_hbm,
-    basis_hbm, norms, estimate,
+    out, norms, estimate,
     u0, u1, u2, u3, u4, u5, u6,
-    fext, cells, small, coef, spread, out, traces, rows,
+    fext, cells, small, coef, spread, traces, rows,
     owners, adjacent, found, table, shuffle, split, coeffs, scales, scales_t, weights, weights2, fw0, bw0, fw1, bw1, parts, inbox,
-    local_sem, halo_send, halo_recv, t_send, t_recv, r_send, r_recv, f_send, f_recv, tp_send, tp_recv, rp_send, rp_recv, out_sem,
+    local_sem, halo_send, halo_recv, t_send, t_recv, r_send, r_recv, f_send, f_recv, tp_send, tp_recv, rp_send, rp_recv,
     s_send, s_recv,
 ):
     x = lax.axis_index("grp")
@@ -366,14 +366,8 @@
             emit(8 + 4 * i + k, k)
         return carry
 
-    quarters = []
-
     def emit_quarter(n):
         lax.fori_loop(2 * n, 2 * n + 2, four_emit, 0)
-        rows_out = pl.ds(8 * n, 8)
-        copy = pltpu.make_async_copy(out.at[rows_out], basis_hbm.at[rows_out], out_sem.at[n])
-        copy.start()
-        quarters.append(copy)
 
     emit_quarter(0)
     spread_out(1)
@@ -463,12 +457,10 @@
     estimate[...] = jnp.sqrt(total + EPS)
     for copy in to_left + to_right + r1 + r2 + r3 + [rp] + list(plane_of.values()) + ahead_of + behind_of + twice + sum(tp, []) + shares:
         copy.wait_send()
-    for copy in quarters:
-        copy.wait()
 
 
 def body(forcing, stiffness, reaction, volumetric, adjacency, owner_map, param_scale, coefficients):
-    anywhere = pl.BlockSpec(memory_space=pl.ANY)
+    anywhere = pl.BlockSpec(memory_space=pltpu.HBM)
     vmem = pl.BlockSpec(memory_space=pltpu.VMEM)
     dma = pltpu.SemaphoreType.DMA
     f32, bf16 = jnp.float32, jnp.bfloat16
@@ -479,12 +471,12 @@
         round_kernel,
         name="round",
         out_shape=(
-            jax.ShapeDtypeStruct((ROWS, 3 * K, Z), bf16),
-            jax.ShapeDtypeStruct((quarter, slots), f32),
-            jax.ShapeDtypeStruct((1, quarter), f32),
+            pltpu.VMEM((ROWS, 3 * K, Z), bf16),
+            pltpu.VMEM((quarter, slots), f32),
+            pltpu.VMEM((1, quarter), f32),
         ),
         in_specs=[anywhere] * 8,
-        out_specs=(anywhere, vmem, vmem),
+        out_specs=(vmem, vmem, vmem),
         scratch_shapes=[pltpu.VMEM((48, 24, 8, Z), f32)] * 7
         + [
             pltpu.VMEM((48, 3 * K, Z), bf16),
@@ -492,7 +484,6 @@
             pltpu.VMEM((56, 2 * Z), f32),
             pltpu.VMEM((7, 48, 2, 8, Z), f32),
             pltpu.VMEM((4, 2, 3 * K // 2, Z), f32),
-            pltpu.VMEM((ROWS, 3 * K, Z), bf16),
             pltpu.VMEM((128, K, Z), bf16),
             pltpu.VMEM((128, 1, Z), f32),
             pltpu.VMEM(owner_map.T.shape, jnp.int32),
@@ -525,7 +516,6 @@
             dma((4, 4)),
             dma,
             dma,
-            dma((4,)),
             dma((npatch - 1,)),
             dma((npatch - 1,)),
         ],

time: 53.8 us -> 51.4 us (0.955)
  local copies, waits for them, and re-layouts: 3.87 us -> 2.31 us
  Pallas kernels: 49.1 us -> 48.3 us
    unnamed x7 -> x3, local copies, waits for them, and re-layouts: 3.87 us -> 2.31 us
    pallas_call x1, Pallas kernels: 49.1 us -> 48.3 us  [body(): pl.pallas_call(round_kernel, name='round', out_shape=(pltpu.VMEM((ROWS, 3...]
where the time goes in v5:
time: 51.4 us; the launch traced here: 51.2 us
  Pallas kernels  48.3 us (94%)
  local copies, waits for them, and re-layouts  2.31 us (4%)
  between operations  0.64 us (1%)
    pallas_call x1, Pallas kernels, body(): pl.pallas_call(round_kernel, name='round', out_shape=(pltpu.VMEM((ROWS, 3...  48.3 us
    unnamed x3, local copies, waits for them, and re-layouts  2.31 us

profile of v5, /device:TPU:1, one launch (start us, length us, event | category | flops | bytes accessed | tf_op | source)
XLA Modules:
  0.0 51.2 jit_solution(10734136299201310878)
XLA Ops:
  0.6 48.3 %round.1 = (bf16[32,192,128]{2,1,0:T(8,128)(2,1)S(1)}, f32[128,256]{1,0:T(8,128)S(1)}, f32[1,128]{1,0:T(1,128)S(1)}) custom-call(bf16[32,192,128]{2,1,0:T(8,128)(2,1)} %bitcast.13, f32[32,128]{1,0:T(8,128)} %bitcast.15, f32[32,128]{1,0:T(8,128)} %bitcast.16, f32[32,128]{1,0:T(8,128)} %bitcast.17, f32[64,512]{1,0:T(8,128)} %bitcast.14, ...), custom_call_target="tpu_custom_call" | custom-call | tf_op jit(solution)/shard_map/round/pallas_call | solution.py:470
  48.9 1.1 %copy.14 = bf16[1,32,192,128]{3,2,1,0:T(8,128)(2,1)} copy(bf16[1,32,192,128]{3,2,1,0:T(8,128)(2,1)S(1)} %bitcast.10) | data formatting | bytes 3145728
  50.1 0.7 %copy.15 = f32[1,128,256]{2,1,0:T(8,128)} copy(f32[1,128,256]{2,1,0:T(8,128)S(1)} %bitcast.11) | data formatting | bytes 262144
  50.7 0.5 copy.16
